TPU v7x, 512 devices: a whole 4x4x16 slice. The times are simulated.
512 devices in a mesh: ep: 128 (over z, x, core), dp: 4 (over y).
Axes of the slice: x: 4, y: 4, z: 16, core: 2. Of those that a mesh axis runs over, the one named last changes fastest.
Arguments:
- tokens: bfloat16 [512, 4096], P(('dp', 'ep')), parts along dimension 0, may hold values from -6 to 6
- expert_ids: int32 [512, 8], P(('dp', 'ep')), parts along dimension 0, may hold values from 0 to 15, as said below
- gates: float32 [512, 8], P(('dp', 'ep')), parts along dimension 0, may hold values from 0.1 to 1
- gate_weight: bfloat16 [128, 192, 4096], P('ep'), may hold values from -0.09375 to 0.09375
- up_weight: bfloat16 [128, 192, 4096], P('ep'), may hold values from -0.09375 to 0.09375
- down_weight: bfloat16 [128, 192, 4096], P('ep'), may hold values from -0.15625 to 0.15625
Outputs:
- combined: bfloat16 [512, 4096], P(('dp', 'ep')), parts along dimension 0
There are 4 independent parts, one for each index of `dp`. A program takes and returns all parts, laid end to end along the dimension named above; an argument that names none is the same for every part. Nothing has to cross between parts.
Inputs may be any that keep to these rules, and one draw needn't show every extreme that they name: `expert_ids`: each row names 8 different experts.
All inputs are finite; a program needn't handle non-finite values.
Results may differ from a plain program's by a relative error of at most 0.012.
Values may be sent and summed in bfloat16 or wider, within the bound.
A program may use at most 64 MiB of HBM per device.

v0:
```python
import jax
import jax.numpy as jnp
from jax import lax
from jax.sharding import PartitionSpec as P

HIDDEN_SIZE = 1536


def shards(tokens, expert_ids, gates, gate_weight, up_weight, down_weight):
    own_rows = tokens.shape[0]
    width = tokens.shape[1]
    devices = lax.axis_size("ep")
    share = HIDDEN_SIZE // gate_weight.shape[1]
    groups = devices // share
    expert_range = jnp.arange(groups, dtype=jnp.int32)
    expert_hits = expert_ids[:, :, None] == expert_range[None, None, :]
    chosen = jnp.any(expert_hits, axis=1)
    send_block = jnp.where(chosen.T[:, :, None], tokens[None, :, :], jnp.zeros((), tokens.dtype))
    weighted = jnp.sum(jnp.where(expert_hits, gates[:, :, None], 0.0), axis=1)
    outgoing = jnp.repeat(send_block, share, axis=0)
    arrived = lax.all_to_all(outgoing, "ep", split_axis=0, concat_axis=0, tiled=True)
    rows_in = arrived.reshape(devices * own_rows, width)
    contract = (((1,), (1,)), ((), ()))
    gate_act = lax.dot_general(
        rows_in, gate_weight[0], contract, preferred_element_type=jnp.float32
    )
    up_act = lax.dot_general(rows_in, up_weight[0], contract, preferred_element_type=jnp.float32)
    hidden = (jax.nn.silu(gate_act) * up_act).astype(jnp.bfloat16)
    partial_value = jnp.dot(hidden, down_weight[0], preferred_element_type=jnp.float32)
    returned = lax.all_to_all(
        partial_value.reshape(devices, own_rows, width),
        "ep",
        split_axis=0,
        concat_axis=0,
        tiled=True,
    )
    expert_out = jnp.sum(returned.reshape(groups, share, own_rows, width), axis=1).astype(
        jnp.bfloat16
    )
    combined = jnp.einsum("re,erd->rd", weighted, expert_out.astype(jnp.float32))
    return combined.astype(jnp.bfloat16)


def solution(mesh):
    return jax.shard_map(
        shards,
        mesh=mesh,
        in_specs=(
            P(("dp", "ep"), None),
            P(("dp", "ep"), None),
            P(("dp", "ep"), None),
            P("ep", None, None),
            P("ep", None, None),
            P("ep", None, None),
        ),
        out_specs=P(("dp", "ep"), None),
        check_vma=False,
    )
```

profile of v0, /device:TPU:24, one launch (start us, length us, event | category | flops | bytes accessed | tf_op | source)
XLA Modules:
  0.0 209.2 jit_solution(11392839661144911835)
XLA Ops:
  0.0 0.0 copy-start
  0.0 0.9 fusion.28
  0.9 0.8 reduce.3
  1.6 0.1 broadcast_select_fusion
  1.7 0.1 broadcast_bitcast_fusion
  1.9 0.5 broadcast.92
  2.4 2.1 %reduce.4 = bf16[128,4096]{1,0:T(8,128)(2,1)} reduce(bf16[128,1,4096]{2,0,1:T(8,128)(2,1)S(1)} %broadcast_bitcast_fusion, bf16[]{:T(256)} %broadcast.92), dimensions={1}, to_apply=%copy.10.reduce_sub_computation | reduce | bytes 2097154 | tf_op jit(solution)/shard_map/broadcast_in_dim | solution.py:20
  4.5 2.6 %reshape.152 = bf16[128,2,2048]{2,1,0:T(2,128)(2,1)} reshape(bf16[128,4096]{1,0:T(8,128)(2,1)} %reduce.4) | data formatting | bytes 2097152
  7.1 73.2 %all_to_all.10 = bf16[128,2,2048]{2,1,0:T(2,128)(2,1)S(1)} all-to-all(bf16[128,2,2048]{2,1,0:T(2,128)(2,1)} %reshape.152), channel_id=1, replica_groups=mesh['ep'=128,'dp'=4] {'ep'}, dimensions={0} | all-to-all | bytes 2097152 | tf_op jit(solution)/shard_map/all_to_all | solution.py:21
  80.3 3.5 %reshape.153 = bf16[128,1,4096]{2,1,0:T(2,128)(2,1)} reshape(bf16[128,2,2048]{2,1,0:T(2,128)(2,1)S(1)} %all_to_all.10) | data formatting | bytes 2097152
  83.8 0.0 copy-start.1
  83.8 3.6 %fusion.3 = f32[128,192]{0,1:T(8,128)S(1)} fusion(bf16[1,192,4096]{2,1,0:T(8,128)(2,1)} %param.9, bf16[128,1,4096]{2,1,0:T(2,128)(2,1)} %reshape.153), kind=kOutput, calls=%fused_computation.5 | convolution fusion | flops 201326592 | bytes 2719744 | tf_op jit(solution)/shard_map/dot_general | solution.py:24
  87.4 0.0 copy-done
  87.4 0.0 copy-done.1
  87.4 5.1 %convolution_bitcast_fusion = f32[128,1,4096]{2,0,1:T(8,128)} fusion(bf16[1,192,4096]{2,1,0:T(8,128)(2,1)S(1)} %copy-done, bf16[1,192,4096]{2,1,0:T(8,128)(2,1)S(1)} %copy-done.1, bf16[128,1,4096]{2,1,0:T(2,128)(2,1)} %reshape.153, f32[128,192]{0,1:T(8,128)S(1)} %fusion.3), kind=kOutput, calls=%fused_computation | convolution fusion | flops 402800640 | bytes 6389760 | tf_op jit(solution)/shard_map/dot_general | solution.py:29
  92.5 5.0 %copy.11 = f32[128,1,4096]{2,1,0:T(1,128)} copy(f32[128,1,4096]{2,0,1:T(8,128)} %convolution_bitcast_fusion) | data formatting | bytes 4194304 | tf_op jit(solution)/shard_map/reshape | solution.py:31
  97.5 0.0 copy-start.2
  97.5 0.0 copy-start.3
  97.5 9.3 %all-to-all-start.1 = ((f32[128,1,4096]{2,1,0:T(1,128)}), f32[128,1,4096]{2,1,0:T(1,128)}, u32[]{:S(2)}, u32[]{:S(2)}) async-start(f32[128,1,4096]{2,1,0:T(1,128)} %copy.11), calls=%async_computation.1 | async-start | bytes 4194304 | tf_op jit(solution)/shard_map/all_to_all | solution.py:30
  106.9 0.0 copy-done.2
  106.9 0.0 copy-done.3
  106.9 0.1 select_reduce_fusion
  107.0 97.7 %all-to-all-done.1 = f32[128,1,4096]{2,1,0:T(1,128)} async-done(((f32[128,1,4096]{2,1,0:T(1,128)}), f32[128,1,4096]{2,1,0:T(1,128)}, u32[]{:S(2)}, u32[]{:S(2)}) %all-to-all-start.1) | async-done | bytes 2097184 | tf_op jit(solution)/shard_map/all_to_all | solution.py:30
  204.7 3.7 %bitcast_reduce_fusion = bf16[16,4096]{1,0:T(8,128)(2,1)S(1)} fusion(f32[128,1,4096]{2,1,0:T(1,128)} %all-to-all-done.1), kind=kLoop, calls=%fused_computation.1 | loop fusion | flops 458752 | bytes 2228224 | tf_op jit(solution)/shard_map/reduce_sum | solution.py:37
  208.4 0.1 fusion.20
  208.5 0.6 convert_element_type.23
  (1 shorter events, 0.0 us)
Async XLA Ops:
  0.0 87.4 %copy-start = (bf16[1,192,4096]{2,1,0:T(8,128)(2,1)S(1)}, bf16[1,192,4096]{2,1,0:T(8,128)(2,1)}, u32[]{:S(2)}) copy-start(bf16[1,192,4096]{2,1,0:T(8,128)(2,1)} %param.11) | copy-start | bytes 4718596
  83.8 3.6 %copy-start.1 = (bf16[1,192,4096]{2,1,0:T(8,128)(2,1)S(1)}, bf16[1,192,4096]{2,1,0:T(8,128)(2,1)}, u32[]{:S(2)}) copy-start(bf16[1,192,4096]{2,1,0:T(8,128)(2,1)} %param.10) | copy-start | bytes 4718596
  97.5 9.3 %copy-start.2 = (s32[1,8]{1,0:T(1,128)S(1)}, s32[1,8]{1,0:T(1,128)}, u32[]{:S(2)}) copy-start(s32[1,8]{1,0:T(1,128)} %param.7) | copy-start | bytes 100
  97.5 9.3 %copy-start.3 = (f32[1,8]{1,0:T(1,128)S(1)}, f32[1,8]{1,0:T(1,128)}, u32[]{:S(2)}) copy-start(f32[1,8]{1,0:T(1,128)} %param.8) | copy-start | bytes 100
  97.5 107.1 %all-to-all-start.1 = ((f32[128,1,4096]{2,1,0:T(1,128)}), f32[128,1,4096]{2,1,0:T(1,128)}, u32[]{:S(2)}, u32[]{:S(2)}) async-start(f32[128,1,4096]{2,1,0:T(1,128)} %copy.11), calls=%async_computation.1 | async-start | bytes 4194304 | tf_op jit(solution)/shard_map/all_to_all | solution.py:30
where the time goes:
time: 210 us; the launch traced here: 209 us
  waiting for transfers between devices  97.7 us (47%)
  blocking collectives  73.2 us (35%)
  local copies, waits for them, and re-layouts  12.4 us (6%)
  starting transfers between devices  9.31 us (4%)
  matrix products  8.85 us (4%)
  other arithmetic  7.61 us (4%)
    all_to_all x1, waiting for transfers between devices, shards(): lax.all_to_all(partial_value.reshape(devices, own_rows, width), 'ep', spl...  97.7 us
    all_to_all x1, blocking collectives, shards(): lax.all_to_all(outgoing, 'ep', split_axis=0, concat_axis=0, tiled=True)  73.2 us
    all_to_all x1, starting transfers between devices, shards(): lax.all_to_all(partial_value.reshape(devices, own_rows, width), 'ep', spl...  9.31 us
    unnamed x10, local copies, waits for them, and re-layouts  6.13 us
    dot_general x1, matrix products, shards(): jnp.dot(hidden, down_weight[0], preferred_element_type=jnp.float32)  5.09 us
    reshape x1, local copies, waits for them, and re-layouts, shards(): partial_value.reshape(devices, own_rows, width)  5.04 us
  transfers between devices with their start and end apart: 1, of which 1 were waited for; matrix products, arithmetic and copies ran while one was open for 0% of the time, Pallas kernels for 0%

commit v1 on v0

v1 whole, which is shorter than its diff:
```python
import functools

import jax
import jax.numpy as jnp
from jax import lax
from jax.experimental import pallas as pl
from jax.experimental.pallas import tpu as pltpu
from jax.sharding import PartitionSpec as P

MESH = pl.DeviceIdType.MESH
F32 = jnp.float32
BF16 = jnp.bfloat16
NZ, NX, NC = 16, 4, 2
SUB, LANE = 32, 128

K_OF = [k for j in range(1, 8) for k in (j, NZ - j)] + [8, 0]
P_OF = {k: p for p, k in enumerate(K_OF)}
NEAR = [(15, 1)] + [(2 * j, 2) for j in range(7)] + [(14, 1)]
FAR = NEAR[::-1]


def kernel(
    tok_ref, ids_ref, gate_ref, wg_hbm, wu_hbm, wd_hbm, out_ref,
    wg, wu, wd, own, got, meta, stage, rows, core_out, core_in, x_out, x_in, x_own, z_out, z_in,
    w_sem, az_s, az_r, am_s, am_r, ax_s, ax_r, ac_s, ac_r, rc_s, rc_r, rx_s, rx_r, rz_s, rz_r,
):
    me = lax.axis_index("ep")
    core = lax.rem(me, NC)
    x = lax.rem(me // NC, NX)
    z = me // (NC * NX)

    def device(dz, dx, dc):
        pz = lax.rem(z + dz, NZ)
        px = lax.rem(x + dx, NX)
        pc = lax.rem(core + dc, NC)
        return {"ep": (pz * NX + px) * NC + pc}

    def send(src, dst, s_sem, r_sem, to):
        copy = pltpu.make_async_remote_copy(
            src_ref=src, dst_ref=dst, send_sem=s_sem, recv_sem=r_sem, device_id=to, device_id_type=MESH
        )
        copy.start()
        return copy

    loads = []
    for n, (src, dst) in enumerate(((wg_hbm, wg), (wu_hbm, wu), (wd_hbm, wd))):
        copy = pltpu.make_async_copy(src.at[0], dst, w_sem.at[n])
        copy.start()
        loads.append(copy)

    peers = [device(k, 0, 0) for k in range(1, NZ)] + [device(0, k, 0) for k in range(1, NX)] + [device(0, 0, 1)]
    barrier = pltpu.get_barrier_semaphore()
    for peer in peers:
        pl.semaphore_signal(barrier, inc=1, device_id=peer, device_id_type=MESH)

    lane = lax.broadcasted_iota(jnp.int32, (1, LANE), 1)
    row = tok_ref[...].astype(F32)
    for j in range(SUB):
        stage[j : j + 1, :] = row[:, j * LANE : (j + 1) * LANE]
    own_row = stage[0:SUB, :].astype(BF16)
    own[...] = own_row
    got[0, 15, 0] = own_row
    weight = jnp.zeros((1, LANE), F32)
    for k in range(ids_ref.shape[1]):
        weight += jnp.where(lane == ids_ref[:, k : k + 1], gate_ref[:, k : k + 1], 0.0)
    meta[15] = weight

    pl.semaphore_wait(barrier, len(peers))

    sends = []
    for d in sorted(range(1, NZ), key=lambda d: -min(d, NZ - d)):
        p = P_OF[NZ - d]
        sends.append(send(own, got.at[0, p, 0], az_s.at[p], az_r.at[p], device(d, 0, 0)))
    for d in sorted(range(1, NZ), key=lambda d: -min(d, NZ - d)):
        p = P_OF[NZ - d]
        sends.append(send(meta.at[15], meta.at[p], am_s.at[p], am_r.at[p], device(d, 0, 0)))

    def take(dst, r_sem):
        pltpu.make_async_copy(dst, dst, r_sem).wait()

    def rows_along_x(g):
        p, n = NEAR[g]
        if g > 0:
            for q in range(p, p + n):
                take(got.at[0, q, 0], az_r.at[q])
        for d in range(1, NX):
            sends.append(
                send(
                    got.at[0, pl.ds(p, n), 0], got.at[0, pl.ds(p, n), NX - d],
                    ax_s.at[g, d - 1], ax_r.at[g, NX - d - 1], device(0, d, 0),
                )
            )

    def rows_to_partner(g):
        p, n = NEAR[g]
        for d in range(1, NX):
            take(got.at[0, pl.ds(p, n), d], ax_r.at[g, d - 1])
        sends.append(send(got.at[0, pl.ds(p, n)], got.at[1, pl.ds(p, n)], ac_s.at[g], ac_r.at[g], device(0, 0, 1)))

    def unpack(side, unit):
        base = side * 64 + unit * 16
        stage[pl.ds(base * SUB, 16 * SUB), :] = (
            got[side, 4 * unit : 4 * unit + 4].astype(F32).reshape(16 * SUB, LANE)
        )
        for j in range(SUB):
            rows[pl.ds(base, 16), j * LANE : (j + 1) * LANE] = stage[
                pl.ds(base * SUB + j, 16, stride=SUB), :
            ].astype(BF16)

    lag = 4
    for g in range(9 + lag):
        if g < 9:
            rows_along_x(g)
        if g >= lag:
            rows_to_partner(g - lag)
    for unit in range(4):
        unpack(0, unit)
    for unit in range(4):
        for g, (p, n) in enumerate(NEAR):
            if p // 4 == unit:
                take(got.at[1, pl.ds(p, n)], ac_r.at[g])
        unpack(1, unit)

    for copy in loads:
        copy.wait()
    contract = (((1,), (1,)), ((), ()))
    gate_act = lax.dot_general(rows[...], wg[...], contract, preferred_element_type=F32)
    up_act = lax.dot_general(rows[...], wu[...], contract, preferred_element_type=F32)
    hidden = (jax.nn.silu(gate_act) * up_act).astype(BF16)
    for n in range(16):
        value = jnp.dot(hidden, wd[:, n * 256 : (n + 1) * 256], preferred_element_type=F32)
        stage[pl.ds(2 * n, 128, stride=SUB), :] = value[:, :LANE]
        stage[pl.ds(2 * n + 1, 128, stride=SUB), :] = value[:, LANE:]

    for g, (p, n) in enumerate(FAR):
        core_out[pl.ds(p, n)] = (
            stage[pl.ds((64 + p * 4) * SUB, n * 4 * SUB), :].astype(BF16).reshape(n, NX, SUB, LANE)
        )
        sends.append(send(core_out.at[pl.ds(p, n)], core_in.at[pl.ds(p, n)], rc_s.at[g], rc_r.at[g], device(0, 0, 1)))
    for g, (p, n) in enumerate(FAR):
        take(core_in.at[pl.ds(p, n)], rc_r.at[g])
        mine = stage[pl.ds(p * 4 * SUB, n * 4 * SUB), :].reshape(n, NX, SUB, LANE)
        both = mine + core_in[pl.ds(p, n)].astype(F32)
        x_own[pl.ds(p, n)] = both[:, 0]
        for d in range(1, NX):
            x_out[d - 1, pl.ds(p, n)] = both[:, d].astype(BF16)
            sends.append(
                send(
                    x_out.at[d - 1, pl.ds(p, n)], x_in.at[NX - d - 1, pl.ds(p, n)],
                    rx_s.at[g, d - 1], rx_r.at[g, NX - d - 1], device(0, d, 0),
                )
            )
    for p in range(15):
        take(meta.at[p], am_r.at[p])
    for g, (p, n) in enumerate(FAR):
        for d in range(1, NX):
            take(x_in.at[d - 1, pl.ds(p, n)], rx_r.at[g, d - 1])
        for q in range(p, p + n):
            total = x_own[q]
            for d in range(1, NX):
                total += x_in[d - 1, q].astype(F32)
            factor = jnp.sum(jnp.where(lane == z, meta[q], 0.0), axis=1, keepdims=True)
            total *= factor
            if q == 15:
                x_own[q] = total
            else:
                k = K_OF[q]
                there = P_OF[NZ - k]
                z_out[q] = total.astype(BF16)
                sends.append(send(z_out.at[q], z_in.at[there], rz_s.at[q], rz_r.at[there], device(k, 0, 0)))
    total = x_own[15]
    for p in range(15):
        take(z_in.at[p], rz_r.at[p])
        total += z_in[p].astype(F32)
    out_ref[...] = total.astype(BF16)
    for copy in sends:
        copy.wait_send()


def shards(tokens, expert_ids, gates, gate_weight, up_weight, down_weight):
    hidden_dev, width = gate_weight.shape[1:]
    sems = pltpu.SemaphoreType.DMA
    vmem = pl.BlockSpec(memory_space=pltpu.VMEM)
    hbm = pl.BlockSpec(memory_space=pl.ANY)
    result = pl.pallas_call(
        kernel,
        name="routed_experts",
        out_shape=jax.ShapeDtypeStruct((SUB, LANE), BF16),
        in_specs=[vmem, vmem, vmem, hbm, hbm, hbm],
        out_specs=vmem,
        scratch_shapes=[
            pltpu.VMEM((hidden_dev, width), BF16),
            pltpu.VMEM((hidden_dev, width), BF16),
            pltpu.VMEM((hidden_dev, width), BF16),
            pltpu.VMEM((SUB, LANE), BF16),
            pltpu.VMEM((NC, NZ, NX, SUB, LANE), BF16),
            pltpu.VMEM((NZ, 1, LANE), F32),
            pltpu.VMEM((128 * SUB, LANE), F32),
            pltpu.VMEM((128, width), BF16),
            pltpu.VMEM((NZ, NX, SUB, LANE), BF16),
            pltpu.VMEM((NZ, NX, SUB, LANE), BF16),
            pltpu.VMEM((NX - 1, NZ, SUB, LANE), BF16),
            pltpu.VMEM((NX - 1, NZ, SUB, LANE), BF16),
            pltpu.VMEM((NZ, SUB, LANE), F32),
            pltpu.VMEM((NZ - 1, SUB, LANE), BF16),
            pltpu.VMEM((NZ - 1, SUB, LANE), BF16),
            sems((3,)),
            sems((15,)), sems((15,)), sems((15,)), sems((15,)),
            sems((9, 3)), sems((9, 3)), sems((9,)), sems((9,)),
            sems((9,)), sems((9,)), sems((9, 3)), sems((9, 3)),
            sems((15,)), sems((15,)),
        ],
        compiler_params=pltpu.CompilerParams(collective_id=0, has_side_effects=True),
    )(tokens, expert_ids, gates, gate_weight, up_weight, down_weight)
    return result.reshape(1, width)


def solution(mesh):
    return jax.shard_map(
        shards,
        mesh=mesh,
        in_specs=(
            P(("dp", "ep"), None),
            P(("dp", "ep"), None),
            P(("dp", "ep"), None),
            P("ep", None, None),
            P("ep", None, None),
            P("ep", None, None),
        ),
        out_specs=P(("dp", "ep"), None),
        check_vma=False,
    )
```

time: 210 us -> 54.5 us (0.26)
  waiting for transfers between devices: 97.7 us -> 0 us
  blocking collectives: 73.2 us -> 0 us
  Pallas kernels: 0 us -> 53 us
  local copies, waits for them, and re-layouts: 12.4 us -> 1.32 us
  starting transfers between devices: 9.31 us -> 0 us
  matrix products: 8.85 us -> 0 us
  other arithmetic: 7.61 us -> 0 us
    all_to_all x1 -> x0, waiting for transfers between devices: 97.7 us -> none  [shards(): lax.all_to_all(partial_value.reshape(devices, own_rows, width), 'ep', spl...]
    all_to_all x1 -> x0, blocking collectives: 73.2 us -> none  [shards(): lax.all_to_all(outgoing, 'ep', split_axis=0, concat_axis=0, tiled=True)]
    pallas_call x0 -> x1, Pallas kernels: none -> 53 us  [shards(): pl.pallas_call(kernel, name='routed_experts', out_shape=jax.ShapeDtypeStr...]
    all_to_all x1 -> x0, starting transfers between devices: 9.31 us -> none  [shards(): lax.all_to_all(partial_value.reshape(devices, own_rows, width), 'ep', spl...]
    dot_general x3 -> x0, matrix products: 8.85 us -> none  [the longest x1 5.09 us: shards(): jnp.dot(hidden, down_weight[0], preferred_element_type=jnp.float32)]
    reshape x1 -> x0, local copies, waits for them, and re-layouts: 5.04 us -> none  [shards(): partial_value.reshape(devices, own_rows, width)]
    unnamed x10 -> x1, local copies, waits for them, and re-layouts: 6.13 us -> 1.32 us
    reduce_sum x2 -> x0, other arithmetic: 3.8 us -> none  [the longest x1 3.71 us: shards(): jnp.sum(returned.reshape(groups, share, own_rows, width), axis=1)]
  transfers between devices with their start and end apart: 1 -> 0, of which waited for: 1 -> 0; matrix products, arithmetic and copies ran while one was open for 0% -> 0% of each run, Pallas kernels for 0% -> 0%
where the time goes in v1:
time: 54.5 us; the launch traced here: 54.3 us
  Pallas kernels  53 us (97%)
  local copies, waits for them, and re-layouts  1.32 us (2%)
    pallas_call x1, Pallas kernels, shards(): pl.pallas_call(kernel, name='routed_experts', out_shape=jax.ShapeDtypeStr...  53 us
    unnamed x1, local copies, waits for them, and re-layouts  1.32 us

profile of v1, /device:TPU:24, one launch (start us, length us, event | category | flops | bytes accessed | tf_op | source)
XLA Modules:
  0.0 54.3 jit_solution(5912991945890767838)
XLA Ops:
  0.0 53.0 %routed_experts.1 = bf16[32,128]{1,0:T(8,128)(2,1)} custom-call(bf16[1,4096]{1,0:T(2,128)(2,1)} %tok_ref.1, s32[1,8]{1,0:T(1,128)} %ids_ref.1, f32[1,8]{1,0:T(1,128)} %gate_ref.1, bf16[1,192,4096]{2,1,0:T(8,128)(2,1)} %wg_hbm.1, bf16[1,192,4096]{2,1,0:T(8,128)(2,1)} %wu_hbm.1, bf16[1,192,4096]{2,1,0:T(8,128)(2,1)} %wd_hbm.1), custom_call_target="tpu_custom_call" | custom-call | tf_op jit(solution)/shard_map/routed_experts/pallas_call | solution.py:185
  53.0 1.3 %copy.9 = bf16[1,1,32,128]{3,1,2,0:T(2,128)(2,1)} copy(bf16[1,1,32,128]{3,2,1,0:T(8,128)(2,1)} %bitcast.5) | data formatting | bytes 16384

commit v2 on v1

--- a/solution.py
+++ b/solution.py
@@ -17,12 +17,18 @@
 P_OF = {k: p for p, k in enumerate(K_OF)}
 NEAR = [(15, 1)] + [(2 * j, 2) for j in range(7)] + [(14, 1)]
 FAR = NEAR[::-1]
+OUT_DIRECT = 2
+BACK_DIRECT = 1
+BACK_LATE = ([(14, 0)] + FAR)[BACK_DIRECT][0]
+SLOTS = 15 - BACK_LATE
+LEG = 3
 
 
 def kernel(
-    tok_ref, ids_ref, gate_ref, wg_hbm, wu_hbm, wd_hbm, out_ref,
-    wg, wu, wd, own, got, meta, stage, rows, core_out, core_in, x_out, x_in, x_own, z_out, z_in,
-    w_sem, az_s, az_r, am_s, am_r, ax_s, ax_r, ac_s, ac_r, rc_s, rc_r, rx_s, rx_r, rz_s, rz_r,
+    tok_hbm, ids_hbm, gate_hbm, wg_hbm, wu_hbm, wd_hbm, out_ref,
+    tok_ref, ids_ref, gate_ref, wg, wu, wd, own, got, meta, stage, rows,
+    core_out, core_in, x_out, x_in, late_out, late_in, x_own, z_out, z_in,
+    w_sem, az_s, az_r, am_s, am_r, ax_s, ax_r, ac_s, ac_r, rc_s, rc_r, rx_s, rx_r, rl_s, rl_r, rz_s, rz_r,
 ):
     me = lax.axis_index("ep")
     core = lax.rem(me, NC)
@@ -42,16 +48,24 @@
         copy.start()
         return copy
 
-    loads = []
-    for n, (src, dst) in enumerate(((wg_hbm, wg), (wu_hbm, wu), (wd_hbm, wd))):
-        copy = pltpu.make_async_copy(src.at[0], dst, w_sem.at[n])
-        copy.start()
-        loads.append(copy)
-
-    peers = [device(k, 0, 0) for k in range(1, NZ)] + [device(0, k, 0) for k in range(1, NX)] + [device(0, 0, 1)]
+    plane = [(dx, dc) for dc in range(NC) for dx in range(NX)][1:]
+    peers = [device(s * d % NZ, 0, 0) for d in range(1, LEG + 1) for s in (1, -1)] + [device(0, dx, dc) for dx, dc in plane]
     barrier = pltpu.get_barrier_semaphore()
     for peer in peers:
         pl.semaphore_signal(barrier, inc=1, device_id=peer, device_id_type=MESH)
+
+    loads = []
+    for n, (src, dst) in enumerate(
+        (
+            (tok_hbm, tok_ref), (ids_hbm, ids_ref), (gate_hbm, gate_ref),
+            (wg_hbm.at[0], wg), (wu_hbm.at[0], wu), (wd_hbm.at[0], wd),
+        )
+    ):
+        copy = pltpu.make_async_copy(src, dst, w_sem.at[n])
+        copy.start()
+        loads.append(copy)
+    for copy in loads[:3]:
+        copy.wait()
 
     lane = lax.broadcasted_iota(jnp.int32, (1, LANE), 1)
     row = tok_ref[...].astype(F32)
@@ -68,33 +82,47 @@
     pl.semaphore_wait(barrier, len(peers))
 
     sends = []
-    for d in sorted(range(1, NZ), key=lambda d: -min(d, NZ - d)):
-        p = P_OF[NZ - d]
-        sends.append(send(own, got.at[0, p, 0], az_s.at[p], az_r.at[p], device(d, 0, 0)))
-    for d in sorted(range(1, NZ), key=lambda d: -min(d, NZ - d)):
-        p = P_OF[NZ - d]
-        sends.append(send(meta.at[15], meta.at[p], am_s.at[p], am_r.at[p], device(d, 0, 0)))
+    for d in range(LEG, 0, -1):
+        for step in (d, NZ - d):
+            p = P_OF[NZ - step]
+            sends.append(send(own, got.at[0, p, 0], az_s.at[p], az_r.at[p], device(step, 0, 0)))
+
+    def gates_along_z():
+        for d in range(1, NZ):
+            p = P_OF[NZ - d]
+            sends.append(send(meta.at[15], meta.at[p], am_s.at[p], am_r.at[p], device(d, 0, 0)))
 
     def take(dst, r_sem):
         pltpu.make_async_copy(dst, dst, r_sem).wait()
 
     def rows_along_x(g):
         p, n = NEAR[g]
-        if g > 0:
+        if g not in (0, LEG):
             for q in range(p, p + n):
                 take(got.at[0, q, 0], az_r.at[q])
-        for d in range(1, NX):
+        for dx, dc in plane if g > 8 - OUT_DIRECT else plane[: NX - 1]:
+            px = (NX - dx) % NX
             sends.append(
                 send(
-                    got.at[0, pl.ds(p, n), 0], got.at[0, pl.ds(p, n), NX - d],
-                    ax_s.at[g, d - 1], ax_r.at[g, NX - d - 1], device(0, d, 0),
+                    got.at[0, pl.ds(p, n), 0], got.at[dc, pl.ds(p, n), px],
+                    ax_s.at[g, dc, dx], ax_r.at[g, dc, px], device(0, dx, dc),
                 )
             )
+
+    def hand_on():
+        below, above = P_OF[NZ - LEG], P_OF[LEG]
+        take(got.at[0, below, 0], az_r.at[below])
+        take(got.at[0, above, 0], az_r.at[above])
+        for m in range(NZ // 2 - LEG, 0, -1):
+            hops = [(below, m)] if LEG + m == NZ // 2 else [(below, m), (above, NZ - m)]
+            for held, step in hops:
+                p = P_OF[(K_OF[held] - step) % NZ]
+                sends.append(send(got.at[0, held, 0], got.at[0, p, 0], az_s.at[p], az_r.at[p], device(step, 0, 0)))
 
     def rows_to_partner(g):
         p, n = NEAR[g]
         for d in range(1, NX):
-            take(got.at[0, pl.ds(p, n), d], ax_r.at[g, d - 1])
+            take(got.at[0, pl.ds(p, n), d], ax_r.at[g, 0, d])
         sends.append(send(got.at[0, pl.ds(p, n)], got.at[1, pl.ds(p, n)], ac_s.at[g], ac_r.at[g], device(0, 0, 1)))
 
     def unpack(side, unit):
@@ -107,21 +135,59 @@
                 pl.ds(base * SUB + j, 16, stride=SUB), :
             ].astype(BF16)
 
-    lag = 4
-    for g in range(9 + lag):
-        if g < 9:
-            rows_along_x(g)
-        if g >= lag:
-            rows_to_partner(g - lag)
-    for unit in range(4):
-        unpack(0, unit)
-    for unit in range(4):
-        for g, (p, n) in enumerate(NEAR):
-            if p // 4 == unit:
-                take(got.at[1, pl.ds(p, n)], ac_r.at[g])
-        unpack(1, unit)
-
-    for copy in loads:
+    def rows_from_partner(g):
+        p, n = NEAR[g]
+        take(got.at[1, pl.ds(p, n)], ac_r.at[g])
+
+    def late_rows(g):
+        p, n = NEAR[g]
+        for dx, dc in plane:
+            take(got.at[dc, pl.ds(p, n), dx], ax_r.at[g, dc, dx])
+
+    rows_along_x(0)
+    rows_along_x(1)
+    rows_along_x(2)
+    hand_on()
+    rows_along_x(3)
+    rows_to_partner(0)
+    rows_to_partner(1)
+    rows_along_x(4)
+    rows_to_partner(2)
+    rows_along_x(5)
+    rows_to_partner(3)
+    rows_along_x(6)
+    rows_along_x(7)
+    rows_along_x(8)
+    gates_along_z()
+    rows_to_partner(4)
+    unpack(0, 0)
+    rows_to_partner(5)
+    unpack(0, 1)
+    rows_to_partner(6)
+    unpack(0, 2)
+    rows_from_partner(1)
+    rows_from_partner(2)
+    unpack(1, 0)
+    rows_from_partner(3)
+    rows_from_partner(4)
+    unpack(1, 1)
+    if OUT_DIRECT < 2:
+        rows_to_partner(7)
+    rows_from_partner(5)
+    rows_from_partner(6)
+    unpack(1, 2)
+    rows_from_partner(0)
+    for g in range(9 - OUT_DIRECT, 9):
+        late_rows(g)
+    unpack(0, 3)
+    if OUT_DIRECT < 2:
+        rows_from_partner(7)
+    if OUT_DIRECT < 1:
+        rows_to_partner(8)
+        rows_from_partner(8)
+    unpack(1, 3)
+
+    for copy in loads[3:]:
         copy.wait()
     contract = (((1,), (1,)), ((), ()))
     gate_act = lax.dot_general(rows[...], wg[...], contract, preferred_element_type=F32)
@@ -132,12 +198,28 @@
         stage[pl.ds(2 * n, 128, stride=SUB), :] = value[:, :LANE]
         stage[pl.ds(2 * n + 1, 128, stride=SUB), :] = value[:, LANE:]
 
+    for g, (p, n) in enumerate(FAR[:BACK_DIRECT]):
+        for dx, dc in plane:
+            px = (NX - dx) % NX
+            for q in range(n):
+                row = ((dc * NZ + p + q) * NX + dx) * SUB
+                late_out[dc, dx, p - BACK_LATE + q] = stage[pl.ds(row, SUB), :].astype(BF16)
+            sends.append(
+                send(
+                    late_out.at[dc, dx, pl.ds(p - BACK_LATE, n)], late_in.at[dc, px, pl.ds(p - BACK_LATE, n)],
+                    rl_s.at[g, dc, dx], rl_r.at[g, dc, px], device(0, dx, dc),
+                )
+            )
     for g, (p, n) in enumerate(FAR):
+        if g < BACK_DIRECT:
+            continue
         core_out[pl.ds(p, n)] = (
             stage[pl.ds((64 + p * 4) * SUB, n * 4 * SUB), :].astype(BF16).reshape(n, NX, SUB, LANE)
         )
         sends.append(send(core_out.at[pl.ds(p, n)], core_in.at[pl.ds(p, n)], rc_s.at[g], rc_r.at[g], device(0, 0, 1)))
     for g, (p, n) in enumerate(FAR):
+        if g < BACK_DIRECT:
+            continue
         take(core_in.at[pl.ds(p, n)], rc_r.at[g])
         mine = stage[pl.ds(p * 4 * SUB, n * 4 * SUB), :].reshape(n, NX, SUB, LANE)
         both = mine + core_in[pl.ds(p, n)].astype(F32)
@@ -153,12 +235,21 @@
     for p in range(15):
         take(meta.at[p], am_r.at[p])
     for g, (p, n) in enumerate(FAR):
-        for d in range(1, NX):
-            take(x_in.at[d - 1, pl.ds(p, n)], rx_r.at[g, d - 1])
+        if g < BACK_DIRECT:
+            for dx, dc in plane:
+                take(late_in.at[dc, dx, pl.ds(p - BACK_LATE, n)], rl_r.at[g, dc, dx])
+        else:
+            for d in range(1, NX):
+                take(x_in.at[d - 1, pl.ds(p, n)], rx_r.at[g, d - 1])
         for q in range(p, p + n):
-            total = x_own[q]
-            for d in range(1, NX):
-                total += x_in[d - 1, q].astype(F32)
+            if g < BACK_DIRECT:
+                total = stage[pl.ds(q * NX * SUB, SUB), :]
+                for dx, dc in plane:
+                    total += late_in[dc, dx, q - BACK_LATE].astype(F32)
+            else:
+                total = x_own[q]
+                for d in range(1, NX):
+                    total += x_in[d - 1, q].astype(F32)
             factor = jnp.sum(jnp.where(lane == z, meta[q], 0.0), axis=1, keepdims=True)
             total *= factor
             if q == 15:
@@ -185,10 +276,13 @@
     result = pl.pallas_call(
         kernel,
         name="routed_experts",
-        out_shape=jax.ShapeDtypeStruct((SUB, LANE), BF16),
-        in_specs=[vmem, vmem, vmem, hbm, hbm, hbm],
+        out_shape=pltpu.VMEM((SUB, LANE), BF16),
+        in_specs=[hbm] * 6,
         out_specs=vmem,
         scratch_shapes=[
+            pltpu.VMEM((1, width), BF16),
+            pltpu.VMEM(expert_ids.shape, jnp.int32),
+            pltpu.VMEM(gates.shape, F32),
             pltpu.VMEM((hidden_dev, width), BF16),
             pltpu.VMEM((hidden_dev, width), BF16),
             pltpu.VMEM((hidden_dev, width), BF16),
@@ -201,13 +295,16 @@
             pltpu.VMEM((NZ, NX, SUB, LANE), BF16),
             pltpu.VMEM((NX - 1, NZ, SUB, LANE), BF16),
             pltpu.VMEM((NX - 1, NZ, SUB, LANE), BF16),
+            pltpu.VMEM((NC, NX, SLOTS, SUB, LANE), BF16),
+            pltpu.VMEM((NC, NX, SLOTS, SUB, LANE), BF16),
             pltpu.VMEM((NZ, SUB, LANE), F32),
             pltpu.VMEM((NZ - 1, SUB, LANE), BF16),
             pltpu.VMEM((NZ - 1, SUB, LANE), BF16),
-            sems((3,)),
+            sems((6,)),
             sems((15,)), sems((15,)), sems((15,)), sems((15,)),
-            sems((9, 3)), sems((9, 3)), sems((9,)), sems((9,)),
+            sems((9, NC, NX)), sems((9, NC, NX)), sems((9,)), sems((9,)),
             sems((9,)), sems((9,)), sems((9, 3)), sems((9, 3)),
+            sems((max(BACK_DIRECT, 1), NC, NX)), sems((max(BACK_DIRECT, 1), NC, NX)),
             sems((15,)), sems((15,)),
         ],
         compiler_params=pltpu.CompilerParams(collective_id=0, has_side_effects=True),

time: 54.5 us -> 46.2 us (0.85)
  Pallas kernels: 53 us -> 45.4 us
  local copies, waits for them, and re-layouts: 1.32 us -> 0.62 us
    pallas_call x1, Pallas kernels: 53 us -> 45.4 us  [shards(): pl.pallas_call(kernel, name='routed_experts', out_shape=pltpu.VMEM((SUB,...]
    unnamed x1, local copies, waits for them, and re-layouts: 1.32 us -> 0.62 us
where the time goes in v2:
time: 46.2 us; the launch traced here: 46 us
  Pallas kernels  45.4 us (98%)
  local copies, waits for them, and re-layouts  0.62 us (1%)
    pallas_call x1, Pallas kernels, shards(): pl.pallas_call(kernel, name='routed_experts', out_shape=pltpu.VMEM((SUB,...  45.4 us

profile of v2, /device:TPU:24, one launch (start us, length us, event | category | flops | bytes accessed | tf_op | source)
XLA Modules:
  0.0 46.0 jit_solution(5554657229794709149)
XLA Ops:
  0.0 45.4 %routed_experts.1 = bf16[32,128]{1,0:T(8,128)(2,1)S(1)} custom-call(bf16[1,4096]{1,0:T(2,128)(2,1)} %tok_hbm.1, s32[1,8]{1,0:T(1,128)} %ids_hbm.1, f32[1,8]{1,0:T(1,128)} %gate_hbm.1, bf16[1,192,4096]{2,1,0:T(8,128)(2,1)} %wg_hbm.1, bf16[1,192,4096]{2,1,0:T(8,128)(2,1)} %wu_hbm.1, bf16[1,192,4096]{2,1,0:T(8,128)(2,1)} %wd_hbm.1), custom_call_target="tpu_custom_call" | custom-call | tf_op jit(solution)/shard_map/routed_experts/pallas_call | solution.py:276
  45.4 0.6 %copy.9 = bf16[1,1,32,128]{3,1,2,0:T(2,128)(2,1)} copy(bf16[1,1,32,128]{3,2,1,0:T(8,128)(2,1)S(1)} %bitcast.5) | data formatting | bytes 16384

commit v3 on v2

--- a/solution.py
+++ b/solution.py
@@ -144,22 +144,14 @@
         for dx, dc in plane:
             take(got.at[dc, pl.ds(p, n), dx], ax_r.at[g, dc, dx])
 
-    rows_along_x(0)
-    rows_along_x(1)
-    rows_along_x(2)
+    for g in range(LEG):
+        rows_along_x(g)
     hand_on()
-    rows_along_x(3)
-    rows_to_partner(0)
-    rows_to_partner(1)
-    rows_along_x(4)
-    rows_to_partner(2)
-    rows_along_x(5)
-    rows_to_partner(3)
-    rows_along_x(6)
-    rows_along_x(7)
-    rows_along_x(8)
+    for g in range(LEG, 9):
+        rows_along_x(g)
     gates_along_z()
-    rows_to_partner(4)
+    for g in range(5):
+        rows_to_partner(g)
     unpack(0, 0)
     rows_to_partner(5)
     unpack(0, 1)
@@ -193,11 +185,18 @@
     gate_act = lax.dot_general(rows[...], wg[...], contract, preferred_element_type=F32)
     up_act = lax.dot_general(rows[...], wu[...], contract, preferred_element_type=F32)
     hidden = (jax.nn.silu(gate_act) * up_act).astype(BF16)
-    for n in range(16):
-        value = jnp.dot(hidden, wd[:, n * 256 : (n + 1) * 256], preferred_element_type=F32)
-        stage[pl.ds(2 * n, 128, stride=SUB), :] = value[:, :LANE]
-        stage[pl.ds(2 * n + 1, 128, stride=SUB), :] = value[:, LANE:]
-
+
+    def down(blocks):
+        size = blocks[0][1] - blocks[0][0]
+        some = jnp.concatenate([hidden[first:last] for first, last in blocks], axis=0)
+        for n in range(16):
+            value = jnp.dot(some, wd[:, n * 256 : (n + 1) * 256], preferred_element_type=F32)
+            for b, (first, _) in enumerate(blocks):
+                part = value[b * size : (b + 1) * size]
+                stage[pl.ds(first * SUB + 2 * n, size, stride=SUB), :] = part[:, :LANE]
+                stage[pl.ds(first * SUB + 2 * n + 1, size, stride=SUB), :] = part[:, LANE:]
+
+    down([(48, 64), (112, 128)])
     for g, (p, n) in enumerate(FAR[:BACK_DIRECT]):
         for dx, dc in plane:
             px = (NX - dx) % NX
@@ -211,6 +210,8 @@
                 )
             )
     for g, (p, n) in enumerate(FAR):
+        if g == 2:
+            down([(0, 48), (64, 112)])
         if g < BACK_DIRECT:
             continue
         core_out[pl.ds(p, n)] = (

time: 46.2 us -> 45.8 us (level)
  Pallas kernels: 45.4 us -> 44.9 us
where the time goes in v3:
time: 45.8 us; the launch traced here: 45.6 us
  Pallas kernels  44.9 us (98%)
  local copies, waits for them, and re-layouts  0.62 us (1%)
    pallas_call x1, Pallas kernels, shards(): pl.pallas_call(kernel, name='routed_experts', out_shape=pltpu.VMEM((SUB,...  44.9 us

profile of v3, /device:TPU:24, one launch (start us, length us, event | category | flops | bytes accessed | tf_op | source)
XLA Modules:
  0.0 45.6 jit_solution(14212765490012240254)
XLA Ops:
  0.0 44.9 %routed_experts.1 = bf16[32,128]{1,0:T(8,128)(2,1)S(1)} custom-call(bf16[1,4096]{1,0:T(2,128)(2,1)} %tok_hbm.1, s32[1,8]{1,0:T(1,128)} %ids_hbm.1, f32[1,8]{1,0:T(1,128)} %gate_hbm.1, bf16[1,192,4096]{2,1,0:T(8,128)(2,1)} %wg_hbm.1, bf16[1,192,4096]{2,1,0:T(8,128)(2,1)} %wu_hbm.1, bf16[1,192,4096]{2,1,0:T(8,128)(2,1)} %wd_hbm.1), custom_call_target="tpu_custom_call" | custom-call | tf_op jit(solution)/shard_map/routed_experts/pallas_call | solution.py:277
  45.0 0.6 %copy.9 = bf16[1,1,32,128]{3,1,2,0:T(2,128)(2,1)} copy(bf16[1,1,32,128]{3,2,1,0:T(8,128)(2,1)S(1)} %bitcast.5) | data formatting | bytes 16384

commit v4 on v3

--- a/solution.py
+++ b/solution.py
@@ -49,6 +49,7 @@
         return copy
 
     plane = [(dx, dc) for dc in range(NC) for dx in range(NX)][1:]
+    late_order = [(2, 1), (2, 0), (1, 1), (3, 1), (1, 0), (3, 0), (0, 1)]
     peers = [device(s * d % NZ, 0, 0) for d in range(1, LEG + 1) for s in (1, -1)] + [device(0, dx, dc) for dx, dc in plane]
     barrier = pltpu.get_barrier_semaphore()
     for peer in peers:
@@ -100,7 +101,7 @@
         if g not in (0, LEG):
             for q in range(p, p + n):
                 take(got.at[0, q, 0], az_r.at[q])
-        for dx, dc in plane if g > 8 - OUT_DIRECT else plane[: NX - 1]:
+        for dx, dc in late_order if g > 8 - OUT_DIRECT else ((2, 0), (1, 0), (3, 0)):
             px = (NX - dx) % NX
             sends.append(
                 send(
@@ -198,7 +199,7 @@
 
     down([(48, 64), (112, 128)])
     for g, (p, n) in enumerate(FAR[:BACK_DIRECT]):
-        for dx, dc in plane:
+        for dx, dc in late_order:
             px = (NX - dx) % NX
             for q in range(n):
                 row = ((dc * NZ + p + q) * NX + dx) * SUB
@@ -225,7 +226,7 @@
         mine = stage[pl.ds(p * 4 * SUB, n * 4 * SUB), :].reshape(n, NX, SUB, LANE)
         both = mine + core_in[pl.ds(p, n)].astype(F32)
         x_own[pl.ds(p, n)] = both[:, 0]
-        for d in range(1, NX):
+        for d in (2, 1, 3):
             x_out[d - 1, pl.ds(p, n)] = both[:, d].astype(BF16)
             sends.append(
                 send(
@@ -260,12 +261,14 @@
                 there = P_OF[NZ - k]
                 z_out[q] = total.astype(BF16)
                 sends.append(send(z_out.at[q], z_in.at[there], rz_s.at[q], rz_r.at[there], device(k, 0, 0)))
+    for copy in sends[:-15]:
+        copy.wait_send()
     total = x_own[15]
     for p in range(15):
         take(z_in.at[p], rz_r.at[p])
         total += z_in[p].astype(F32)
     out_ref[...] = total.astype(BF16)
-    for copy in sends:
+    for copy in sends[-15:]:
         copy.wait_send()
 
 

time: 45.8 us -> 45.7 us (level)
  no operation moved by 1% of the time
where the time goes in v4:
time: 45.7 us; the launch traced here: 45.4 us
  Pallas kernels  44.8 us (98%)
  local copies, waits for them, and re-layouts  0.62 us (1%)
    pallas_call x1, Pallas kernels, shards(): pl.pallas_call(kernel, name='routed_experts', out_shape=pltpu.VMEM((SUB,...  44.8 us

profile of v4, /device:TPU:24, one launch (start us, length us, event | category | flops | bytes accessed | tf_op | source)
XLA Modules:
  0.0 45.4 jit_solution(13943560382403584013)
XLA Ops:
  0.0 44.8 %routed_experts.1 = bf16[32,128]{1,0:T(8,128)(2,1)S(1)} custom-call(bf16[1,4096]{1,0:T(2,128)(2,1)} %tok_hbm.1, s32[1,8]{1,0:T(1,128)} %ids_hbm.1, f32[1,8]{1,0:T(1,128)} %gate_hbm.1, bf16[1,192,4096]{2,1,0:T(8,128)(2,1)} %wg_hbm.1, bf16[1,192,4096]{2,1,0:T(8,128)(2,1)} %wu_hbm.1, bf16[1,192,4096]{2,1,0:T(8,128)(2,1)} %wd_hbm.1), custom_call_target="tpu_custom_call" | custom-call | tf_op jit(solution)/shard_map/routed_experts/pallas_call | solution.py:280
  44.8 0.6 %copy.9 = bf16[1,1,32,128]{3,1,2,0:T(2,128)(2,1)} copy(bf16[1,1,32,128]{3,2,1,0:T(8,128)(2,1)S(1)} %bitcast.5) | data formatting | bytes 16384

commit v5 on v4

--- a/solution.py
+++ b/solution.py
@@ -293,7 +293,7 @@
             pltpu.VMEM((SUB, LANE), BF16),
             pltpu.VMEM((NC, NZ, NX, SUB, LANE), BF16),
             pltpu.VMEM((NZ, 1, LANE), F32),
-            pltpu.VMEM((128 * SUB, LANE), F32),
+            pltpu.VMEM((129 * SUB, LANE), F32),
             pltpu.VMEM((128, width), BF16),
             pltpu.VMEM((NZ, NX, SUB, LANE), BF16),
             pltpu.VMEM((NZ, NX, SUB, LANE), BF16),

time: 45.7 us -> 45.7 us (level)
  no operation moved by 1% of the time
where the time goes in v5:
time: 45.7 us; the launch traced here: 45.4 us
  Pallas kernels  44.8 us (98%)
  local copies, waits for them, and re-layouts  0.62 us (1%)
    pallas_call x1, Pallas kernels, shards(): pl.pallas_call(kernel, name='routed_experts', out_shape=pltpu.VMEM((SUB,...  44.8 us

profile of v5, /device:TPU:24, one launch (start us, length us, event | category | flops | bytes accessed | tf_op | source)
XLA Modules:
  0.0 45.4 jit_solution(8917466503205157945)
XLA Ops:
  0.0 44.8 %routed_experts.1 = bf16[32,128]{1,0:T(8,128)(2,1)S(1)} custom-call(bf16[1,4096]{1,0:T(2,128)(2,1)} %tok_hbm.1, s32[1,8]{1,0:T(1,128)} %ids_hbm.1, f32[1,8]{1,0:T(1,128)} %gate_hbm.1, bf16[1,192,4096]{2,1,0:T(8,128)(2,1)} %wg_hbm.1, bf16[1,192,4096]{2,1,0:T(8,128)(2,1)} %wu_hbm.1, bf16[1,192,4096]{2,1,0:T(8,128)(2,1)} %wd_hbm.1), custom_call_target="tpu_custom_call" | custom-call | tf_op jit(solution)/shard_map/routed_experts/pallas_call | solution.py:280
  44.8 0.6 %copy.9 = bf16[1,1,32,128]{3,1,2,0:T(2,128)(2,1)} copy(bf16[1,1,32,128]{3,2,1,0:T(8,128)(2,1)S(1)} %bitcast.5) | data formatting | bytes 16384

commit v6 on v4

--- a/solution.py
+++ b/solution.py
@@ -236,6 +236,7 @@
             )
     for p in range(15):
         take(meta.at[p], am_r.at[p])
+    factors = [jnp.sum(jnp.where(lane == z, meta[p], 0.0), axis=1, keepdims=True) for p in range(NZ)]
     for g, (p, n) in enumerate(FAR):
         if g < BACK_DIRECT:
             for dx, dc in plane:
@@ -252,8 +253,7 @@
                 total = x_own[q]
                 for d in range(1, NX):
                     total += x_in[d - 1, q].astype(F32)
-            factor = jnp.sum(jnp.where(lane == z, meta[q], 0.0), axis=1, keepdims=True)
-            total *= factor
+            total *= factors[q]
             if q == 15:
                 x_own[q] = total
             else:

time: 45.7 us -> 45.9 us (level)
  no operation moved by 1% of the time
where the time goes in v6:
time: 45.9 us; the launch traced here: 45.4 us
  Pallas kernels  44.7 us (97%)
  local copies, waits for them, and re-layouts  0.62 us (1%)
    pallas_call x1, Pallas kernels, shards(): pl.pallas_call(kernel, name='routed_experts', out_shape=pltpu.VMEM((SUB,...  44.7 us

profile of v6, /device:TPU:24, one launch (start us, length us, event | category | flops | bytes accessed | tf_op | source)
XLA Modules:
  0.0 45.4 jit_solution(3194934621168406513)
XLA Ops:
  0.0 44.7 %routed_experts.1 = bf16[32,128]{1,0:T(8,128)(2,1)S(1)} custom-call(bf16[1,4096]{1,0:T(2,128)(2,1)} %tok_hbm.1, s32[1,8]{1,0:T(1,128)} %ids_hbm.1, f32[1,8]{1,0:T(1,128)} %gate_hbm.1, bf16[1,192,4096]{2,1,0:T(8,128)(2,1)} %wg_hbm.1, bf16[1,192,4096]{2,1,0:T(8,128)(2,1)} %wu_hbm.1, bf16[1,192,4096]{2,1,0:T(8,128)(2,1)} %wd_hbm.1), custom_call_target="tpu_custom_call" | custom-call | tf_op jit(solution)/shard_map/routed_experts/pallas_call | solution.py:280
  44.7 0.6 %copy.9 = bf16[1,1,32,128]{3,1,2,0:T(2,128)(2,1)} copy(bf16[1,1,32,128]{3,2,1,0:T(8,128)(2,1)S(1)} %bitcast.5) | data formatting | bytes 16384
